TPU v7x, 256 devices: a whole 4x4x8 slice. The times are simulated.
256 devices in a mesh: ctx: 16 (over y, x), exp: 16 (over z, core).
Axes of the slice: x: 4, y: 4, z: 8, core: 2. Of those that a mesh axis runs over, the one named last changes fastest.
Arguments:
- tokens: bfloat16 [2048, 4096], P('ctx', 'exp'), may hold values from -6 to 6
- input_weight: bfloat16 [4096, 8192], P('ctx', 'exp'), may hold values from -0.09375 to 0.09375
- gate_weight: bfloat16 [4096, 8192], P('ctx', 'exp'), may hold values from -0.09375 to 0.09375
- conv_weight: float32 [4, 8192], P(None, 'exp'), may hold values from -3 to 3
- conv_bias: float32 [8192], P('exp'), may hold values from -3 to 3
- state_weight: bfloat16 [8192, 32], P('exp'), may hold values from -0.0078125 to 0.0078125
- step_size: float32 [2048, 8192], P('ctx', 'exp'), may hold values from 0 to 1, as said below
- skip_gain: float32 [8192], P('exp'), may hold values from 0.5 to 2
- output_weight: bfloat16 [8192, 4096], P('exp', 'ctx'), may hold values from -0.0625 to 0.0625
- norm_gain: float32 [4096], replicated, may hold values from 0.1 to 1.9
- router_weight: bfloat16 [4096, 16], replicated, may hold values from -0.09375 to 0.09375
- expert_gate: bfloat16 [16, 7168, 4096], P('exp', 'ctx'), may hold values from -0.09375 to 0.09375
- expert_up: bfloat16 [16, 7168, 4096], P('exp', 'ctx'), may hold values from -0.09375 to 0.09375
- expert_down: bfloat16 [16, 7168, 4096], P('exp', 'ctx'), may hold values from -0.0625 to 0.0625
- expert_ids: int32 [2048, 2], P(('ctx', 'exp')), may hold values from 0 to 15, all different within a row; in each aligned block of 8 rows (0 to 7, 8 to 15, ...) at most 2 rows name the same one
Outputs:
- layer_out: bfloat16 [2048, 4096], P(('ctx', 'exp'))
Inputs may be any that keep to these rules, and one draw needn't show every extreme that they name: `expert_ids`: each token names 2 different experts; in each aligned block of 8 tokens no expert is named by more than 2 tokens. `step_size`: a positive rate for each token and channel.
All inputs are finite; a program needn't handle non-finite values.
Results may differ from a plain program's by a relative error of at most 0.028.
Values may be sent and summed in bfloat16 or wider, within the bound.
A program may use at most 128 MiB of HBM per device.

v0:
```python
import jax
import jax.numpy as jnp
from jax import lax
from jax.sharding import PartitionSpec as P

STATE = 16
CONV = 4
TOP = 2
CAP = 2
precise = lax.Precision.HIGHEST


def shifted(shard, axis, by):
    devices = lax.axis_size(axis)
    pairs = [(i, i + by) for i in range(devices) if 0 <= i + by < devices]
    return lax.ppermute(shard, axis, pairs)


def running_sum(values):
    length = values.shape[0]
    lower = jnp.tril(jnp.ones((length, length), jnp.float32))
    return jnp.dot(lower, values, precision=precise)


def causal_part(scores, decay_block, input_block):
    length = decay_block.shape[0]
    causal = (jnp.arange(length)[:, None] >= jnp.arange(length)[None, :])[:, :, None]
    distance = decay_block[:, None, :] - decay_block[None, :, :]
    weight = jnp.where(causal, jnp.exp(-jnp.where(causal, distance, 0.0)), 0.0)
    return jnp.einsum("ts,tsc,sc->tc", scores, weight, input_block, precision=precise)


def local(
    tokens,
    input_weight,
    gate_weight,
    conv_weight,
    conv_bias,
    state_weight,
    step_size,
    skip_gain,
    output_weight,
    norm_gain,
    router_weight,
    expert_gate,
    expert_up,
    expert_down,
    expert_ids,
):
    whole_stretch = lax.all_gather(tokens, "exp", axis=1, tiled=True)
    stretch_rows = whole_stretch.shape[0]
    inner_width = input_weight.shape[1]
    inner_x = jnp.dot(
        whole_stretch,
        lax.all_gather(input_weight, "ctx", axis=0, tiled=True),
        preferred_element_type=jnp.float32,
    )
    inner_z = jnp.dot(
        whole_stretch,
        lax.all_gather(gate_weight, "ctx", axis=0, tiled=True),
        preferred_element_type=jnp.float32,
    )
    inner_x = inner_x.astype(jnp.bfloat16)
    inner_z = inner_z.astype(jnp.bfloat16)
    earlier_rows = shifted(inner_x[stretch_rows - (CONV - 1) :], "ctx", 1)
    extended = jnp.concatenate([earlier_rows, inner_x], 0).astype(jnp.float32)
    filtered = jnp.broadcast_to(conv_bias[None, :], (stretch_rows, inner_width))
    for offset in range(CONV):
        filtered = (
            filtered + conv_weight[offset][None, :] * extended[offset : offset + stretch_rows]
        )
    mixer_in = jax.nn.silu(filtered).astype(jnp.bfloat16)
    mixer_wide = mixer_in.astype(jnp.float32)
    projections = lax.psum(
        jnp.dot(mixer_in, state_weight, preferred_element_type=jnp.float32), "exp"
    )
    input_gain = projections[:, :STATE]
    readout = projections[:, STATE:]
    cumulative = running_sum(step_size)
    scores = jnp.dot(readout, input_gain.T, precision=precise)
    block_width = 128
    block_count = inner_width // block_width
    decay_blocks = cumulative.reshape(stretch_rows, block_count, block_width).transpose(1, 0, 2)
    incoming_slabs = mixer_wide.reshape(stretch_rows, block_count, block_width).transpose(1, 0, 2)
    inside = lax.map(
        lambda paired: causal_part(scores, paired[0], paired[1]), (decay_blocks, incoming_slabs)
    )
    inside = inside.transpose(1, 0, 2).reshape(stretch_rows, inner_width)
    total_decay = cumulative[stretch_rows - 1]
    tail_weight = jnp.exp(-(total_decay[None, :] - cumulative)) * mixer_wide
    local_end = jnp.dot(tail_weight.T, input_gain, precision=precise)
    stretch_keep = jnp.exp(-total_decay)

    def relay_step(turn_index, received):
        leaving = stretch_keep[:, None] * received + local_end
        return shifted(leaving, "ctx", 1)

    entering = lax.fori_loop(0, lax.axis_size("ctx") - 1, relay_step, jnp.zeros_like(local_end))
    carried = jnp.exp(-cumulative) * jnp.dot(readout, entering.T, precision=precise)
    mixed_state = (inside + carried + skip_gain[None, :] * mixer_wide) * jax.nn.silu(
        inner_z.astype(jnp.float32)
    )
    blender_result = mixed_state.astype(jnp.bfloat16)
    row_count = expert_ids.shape[0]
    start_row = lax.axis_index("exp") * row_count
    own_tokens = lax.dynamic_slice_in_dim(whole_stretch, start_row, row_count, 0)
    out_whole = lax.all_gather(output_weight, "ctx", axis=1, tiled=True)
    projected = lax.psum_scatter(
        jnp.dot(blender_result, out_whole, preferred_element_type=jnp.float32).astype(jnp.bfloat16),
        "exp",
        scatter_dimension=0,
        tiled=True,
    ).astype(jnp.float32)
    residual = (own_tokens.astype(jnp.float32) + projected).astype(jnp.bfloat16)
    stream = residual.astype(jnp.float32)
    normed = (
        stream
        * lax.rsqrt(jnp.mean(stream * stream, -1, keepdims=True) + 1e-05)
        * norm_gain[None, :]
    ).astype(jnp.bfloat16)
    logits = jnp.dot(normed, router_weight, preferred_element_type=jnp.float32)
    experts = router_weight.shape[1]
    expert_range = jnp.arange(experts, dtype=jnp.int32)
    chosen = expert_ids[:, :, None] == expert_range[None, None, :]
    selected_entry = jnp.sum(jnp.where(chosen, logits[:, None, :], 0.0), -1)
    shares = jax.nn.sigmoid(selected_entry - selected_entry[:, ::-1])
    flat_hits = chosen.reshape(row_count * TOP, experts).astype(jnp.int32)
    earlier_hits = jnp.dot(
        jnp.tril(jnp.ones((row_count * TOP, row_count * TOP), jnp.float32), -1),
        flat_hits.astype(jnp.float32),
        precision=precise,
    ).astype(jnp.int32)
    slot_index = jnp.sum(earlier_hits * flat_hits, -1)
    target = expert_ids.reshape(-1) * CAP + slot_index
    placed = target[:, None] == jnp.arange(experts * CAP, dtype=jnp.int32)[None, :]
    placed = placed.reshape(row_count, TOP, experts * CAP)
    selector = jnp.any(placed, 1).astype(jnp.bfloat16)
    outgoing = lax.dot_general(
        selector, normed, (((0,), (0,)), ((), ())), preferred_element_type=jnp.float32
    ).astype(jnp.bfloat16)
    outgoing = outgoing.reshape(experts, CAP, -1)
    arrived = lax.all_to_all(outgoing, "exp", split_axis=0, concat_axis=0, tiled=True)
    arrived = arrived.reshape(-1, arrived.shape[2])
    gate_part = expert_gate[0]
    up_part = expert_up[0]
    down_part = expert_down[0]
    shard_rows = lax.all_gather(arrived, "ctx", axis=0, tiled=True)
    gate_value = lax.dot_general(
        shard_rows, gate_part, (((1,), (1,)), ((), ())), preferred_element_type=jnp.float32
    )
    up_value = lax.dot_general(
        shard_rows, up_part, (((1,), (1,)), ((), ())), preferred_element_type=jnp.float32
    )
    hidden = (jax.nn.silu(gate_value) * up_value).astype(jnp.bfloat16)
    partial_out = jnp.dot(hidden, down_part, preferred_element_type=jnp.float32)
    finished = lax.psum_scatter(
        partial_out.astype(jnp.bfloat16), "ctx", scatter_dimension=0, tiled=True
    )
    returned = lax.all_to_all(
        finished.reshape(experts, CAP, -1), "exp", split_axis=0, concat_axis=0, tiled=True
    )
    returned = returned.reshape(experts * CAP, -1).astype(jnp.float32)
    combine = jnp.sum(jnp.where(placed, shares[:, :, None], 0.0), 1)
    moe_out = jnp.dot(combine, returned, precision=precise)
    return (stream + moe_out).astype(jnp.bfloat16)


def solution(mesh):
    in_specs = (
        P("ctx", "exp"),
        P("ctx", "exp"),
        P("ctx", "exp"),
        P(None, "exp"),
        P("exp"),
        P("exp", None),
        P("ctx", "exp"),
        P("exp"),
        P("exp", "ctx"),
        P(),
        P(),
        P("exp", "ctx", None),
        P("exp", "ctx", None),
        P("exp", "ctx", None),
        P(("ctx", "exp"), None),
    )
    out_specs = P(("ctx", "exp"), None)
    return jax.shard_map(local, mesh=mesh, in_specs=in_specs, out_specs=out_specs, check_vma=False)
```

profile of v0, /device:TPU:1, one launch (start us, length us, event | category | flops | bytes accessed | tf_op | source)
XLA Modules:
  0.0 636.4 jit_solution(114218375562185634)
XLA Ops:
  6.5 0.7 all-gather.6.cloned.1.call-update
  7.3 0.7 all-gather.8.cloned.1.call-update
  8.1 0.7 all-gather.10.cloned.1.call-update
  8.8 0.5 all-gather.12.cloned.1.call-update
  9.4 0.9 fusion.69
  10.2 0.4 fusion.45
  10.6 40.3 %all-gather.6.cloned.1.call-done = bf16[128,4096]{1,0:T(8,128)(2,1)} async-done(((bf16[128,256]{1,0:T(8,128)(2,1)}), bf16[128,4096]{1,0:T(8,128)(2,1)}) %all-gather.6.cloned.1.call-update) | async-done | bytes 1048592 | tf_op jit(solution)/shard_map/all_gather | solution.py:50
  51.0 57.7 %all-gather.8.cloned.1.call-done = bf16[4096,512]{1,0:T(8,128)(2,1)} async-done(((bf16[256,512]{1,0:T(8,128)(2,1)}), bf16[4096,512]{1,0:T(8,128)(2,1)}) %all-gather.8.cloned.1.call-update) | async-done | bytes 4194320 | tf_op jit(solution)/shard_map/all_gather | solution.py:55
  108.7 3.2 convolution_convert_fusion.4
  112.0 3.1 collective-permute-start.1
  115.1 52.4 %all-gather.10.cloned.1.call-done = bf16[4096,512]{1,0:T(8,128)(2,1)} async-done(((bf16[256,512]{1,0:T(8,128)(2,1)}), bf16[4096,512]{1,0:T(8,128)(2,1)}) %all-gather.10.cloned.1.call-update) | async-done | bytes 4194320 | tf_op jit(solution)/shard_map/all_gather | solution.py:60
  167.4 2.9 fusion.30
  170.7 46.7 %psum.7 = f32[128,32]{0,1:T(8,128)S(1)} all-reduce(f32[128,32]{0,1:T(8,128)S(1)} %fusion.70), channel_id=1, replica_groups=mesh['ctx'=16,'exp'=16] {'exp'}, use_global_device_ids=true, to_apply=%region_0.1 | all-reduce | flops 4096 | bytes 32768 | tf_op jit(solution)/shard_map/psum | solution.py:74
  217.7 0.3 fusion.33
  218.1 39.1 %while.20 = (s32[]{:T(128)}, f32[4,128,128]{2,1,0:T(8,128)S(1)}, f32[4,128,128]{2,1,0:T(8,128)S(1)}, f32[4,128,128]{2,1,0:T(8,128)S(1)}, f32[128,128]{1,0:T(8,128)S(1)}, /*index=5*/s32[]{:T(128)}) while((s32[]{:T(128)}, f32[4,128,128]{2,1,0:T(8,128)S(1)}, f32[4,128,128]{2,1,0:T(8,128)S(1)}, f32[4,128,128]{2,1,0:T(8,128)S(1)}, ...), condition=%wide.region_2.3_spmd, body=%wide.region_1.2_spmd.sunk | while | flops 35667968 | bytes 688205 | solution.py:85
  218.1 9.7 %fusion.104 = f32[128,1,128]{2,1,0:T(1,128)S(1)} fusion(f32[128,128,1]{1,2,0:T(1,128)S(1)} %bitcast.89, f32[128,128]{1,0:T(8,128)S(1)} %get-tuple-element.140, f32[128,128]{1,0:T(8,128)S(1)} %get-tuple-element.141, pred[128,128]{1,0:T(8,128)(4,1)S(1)} %iota_compare_fusion.10), kind=kOutput, calls=%fused_computation.clone.1 | convolution fusion | flops 35651584 | bytes 278528 | tf_op jit(solution)/shard_map/while/body/eval_jaxpr/ts,tsc,sc->tc/dot_general | solution.py:30
  227.9 9.7 %fusion.104 = f32[128,1,128]{2,1,0:T(1,128)S(1)} fusion(f32[128,128,1]{1,2,0:T(1,128)S(1)} %bitcast.89, f32[128,128]{1,0:T(8,128)S(1)} %get-tuple-element.140, f32[128,128]{1,0:T(8,128)S(1)} %get-tuple-element.141, pred[128,128]{1,0:T(8,128)(4,1)S(1)} %iota_compare_fusion.10), kind=kOutput, calls=%fused_computation.clone.1 | convolution fusion | flops 35651584 | bytes 278528 | tf_op jit(solution)/shard_map/while/body/eval_jaxpr/ts,tsc,sc->tc/dot_general | solution.py:30
  237.6 9.7 %fusion.104 = f32[128,1,128]{2,1,0:T(1,128)S(1)} fusion(f32[128,128,1]{1,2,0:T(1,128)S(1)} %bitcast.89, f32[128,128]{1,0:T(8,128)S(1)} %get-tuple-element.140, f32[128,128]{1,0:T(8,128)S(1)} %get-tuple-element.141, pred[128,128]{1,0:T(8,128)(4,1)S(1)} %iota_compare_fusion.10), kind=kOutput, calls=%fused_computation.clone.1 | convolution fusion | flops 35651584 | bytes 278528 | tf_op jit(solution)/shard_map/while/body/eval_jaxpr/ts,tsc,sc->tc/dot_general | solution.py:30
  247.4 9.7 %fusion.104 = f32[128,1,128]{2,1,0:T(1,128)S(1)} fusion(f32[128,128,1]{1,2,0:T(1,128)S(1)} %bitcast.89, f32[128,128]{1,0:T(8,128)S(1)} %get-tuple-element.140, f32[128,128]{1,0:T(8,128)S(1)} %get-tuple-element.141, pred[128,128]{1,0:T(8,128)(4,1)S(1)} %iota_compare_fusion.10), kind=kOutput, calls=%fused_computation.clone.1 | convolution fusion | flops 35651584 | bytes 278528 | tf_op jit(solution)/shard_map/while/body/eval_jaxpr/ts,tsc,sc->tc/dot_general | solution.py:30
  257.1 90.6 %while.21 = (s32[]{:T(128)}, f32[512,16]{0,1:T(8,128)S(1)}, f32[512]{0:T(512)S(1)}, f32[512,16]{0,1:T(8,128)S(1)}, s32[]{:T(128)}) while((s32[]{:T(128)}, f32[512,16]{0,1:T(8,128)S(1)}, f32[512]{0:T(512)S(1)}, f32[512,16]{0,1:T(8,128)S(1)}, s32[]{:T(128)}) %tuple.40), condition=%wide.region_4.5_spmd, body=%wide.region_3.4_spmd.sunk | while | flops 16386 | bytes 231525 | solution.py:98
  257.2 2.7 collective-permute-start
  259.9 1.0 collective-permute-done
  260.9 3.6 collective-permute-start
  264.5 1.0 collective-permute-done
  265.5 3.6 collective-permute-start
  269.2 1.0 collective-permute-done
  270.2 4.0 collective-permute-start
  274.3 1.0 collective-permute-done
  275.3 3.7 collective-permute-start
  279.0 1.0 collective-permute-done
  280.0 5.8 collective-permute-start
  285.8 1.0 collective-permute-done
  286.8 5.7 collective-permute-start
  292.5 1.0 collective-permute-done
  293.5 5.8 collective-permute-start
  299.3 1.0 collective-permute-done
  300.3 5.8 collective-permute-start
  306.1 1.0 collective-permute-done
  307.1 5.8 collective-permute-start
  312.8 1.0 collective-permute-done
  313.8 5.8 collective-permute-start
  319.6 1.0 collective-permute-done
  320.6 5.8 collective-permute-start
  326.4 1.2 collective-permute-done
  327.6 5.6 collective-permute-start
  333.1 1.0 collective-permute-done
  334.2 5.8 collective-permute-start
  339.9 1.0 collective-permute-done
  340.9 5.8 collective-permute-start
  346.7 1.0 collective-permute-done
  347.7 0.5 fusion.29
  348.2 3.9 convolution_convert_fusion.1
  352.9 81.1 %reduce-scatter.3.cloned.1.call-done = bf16[8,4096]{1,0:T(8,128)(2,1)} async-done(((bf16[128,4096]{1,0:T(8,128)(2,1)}), bf16[8,4096]{1,0:T(8,128)(2,1)}) %reduce-scatter.3.cloned.1.call-update) | async-done | bytes 65552 | tf_op jit(solution)/shard_map/reduce_scatter | solution.py:108
  434.0 1.0 fusion.41
  435.4 19.1 %all_to_all.10 = bf16[16,2,4096]{2,1,0:T(2,128)(2,1)S(1)} all-to-all(bf16[16,2,4096]{2,1,0:T(2,128)(2,1)S(1)} %reshape.74), channel_id=1, replica_groups=mesh['ctx'=16,'exp'=16] {'exp'}, dimensions={0} | all-to-all | bytes 524288 | tf_op jit(solution)/shard_map/all_to_all | solution.py:142
  454.5 0.8 reshape.75
  455.6 53.0 %all-gather.14.cloned.1.call-done = bf16[512,4096]{1,0:T(8,128)(2,1)} async-done(((bf16[32,4096]{1,0:T(8,128)(2,1)}), bf16[512,4096]{1,0:T(8,128)(2,1)}) %all-gather.14.cloned.1.call-update) | async-done | bytes 4194320 | tf_op jit(solution)/shard_map/all_gather | solution.py:147
  508.6 5.4 fusion.18
  514.0 10.8 %convolution_convert_fusion = bf16[512,4096]{1,0:T(8,128)(2,1)} fusion(bf16[1,448,4096]{2,1,0:T(8,128)(2,1)} %param.32, bf16[512,4096]{1,0:T(8,128)(2,1)} %all-gather.14.cloned.1.call-done, bf16[1,448,4096]{2,1,0:T(8,128)(2,1)} %param.31, f32[512,448]{0,1:T(8,128)S(1)} %fusion.18), kind=kOutput, calls=%fused_computation.19 | convolution fusion | flops 3761569792 | bytes 16646144 | tf_op jit(solution)/shard_map/dot_general | solution.py:155
  524.8 80.9 %reduce-scatter.5.cloned.1.call-done = bf16[32,4096]{1,0:T(8,128)(2,1)} async-done(((bf16[512,4096]{1,0:T(8,128)(2,1)}), bf16[32,4096]{1,0:T(8,128)(2,1)}) %reduce-scatter.5.cloned.1.call-update) | async-done | bytes 262160 | tf_op jit(solution)/shard_map/reduce_scatter | solution.py:156
  605.7 1.8 reshape.76
  607.5 9.4 %all-to-all-start.1 = ((bf16[16,2,4096]{2,1,0:T(2,128)(2,1)}), bf16[16,2,4096]{2,1,0:T(2,128)(2,1)S(1)}, u32[]{:S(2)}, u32[]{:S(2)}) async-start(bf16[16,2,4096]{2,1,0:T(2,128)(2,1)} %reshape.76), calls=%async_computation.3 | async-start | bytes 524288 | tf_op jit(solution)/shard_map/all_to_all | solution.py:159
  617.4 11.2 %all-to-all-done.1 = bf16[16,2,4096]{2,1,0:T(2,128)(2,1)S(1)} async-done(((bf16[16,2,4096]{2,1,0:T(2,128)(2,1)}), bf16[16,2,4096]{2,1,0:T(2,128)(2,1)S(1)}, u32[]{:S(2)}, u32[]{:S(2)}) %all-to-all-start.1) | async-done | bytes 262176 | tf_op jit(solution)/shard_map/all_to_all | solution.py:159
  628.7 0.9 fusion.14
  (82 shorter events, 3.2 us)
Async XLA Ops:
  6.5 3.7 copy-start
  6.5 44.5 %all-gather.6.cloned.1.call-start = ((), (), s32[]{:S(2)}) async-start(), calls=%async_computation.4 | async-start | bytes 1114112 | tf_op jit(solution)/shard_map/all_gather | solution.py:50
  7.3 101.4 %all-gather.8.cloned.1.call-start = ((), (), s32[]{:S(2)}) async-start(), calls=%async_computation.5 | async-start | bytes 4456448 | tf_op jit(solution)/shard_map/all_gather | solution.py:55
  8.0 159.4 %all-gather.10.cloned.1.call-start = ((), (), s32[]{:S(2)}) async-start(), calls=%async_computation.6 | async-start | bytes 4456448 | tf_op jit(solution)/shard_map/all_gather | solution.py:60
  8.7 339.5 %all-gather.12.cloned.1.call-start = ((), (), s32[]{:S(2)}) async-start(), calls=%async_computation.7 | async-start | bytes 4456448 | tf_op jit(solution)/shard_map/all_gather | solution.py:107
  9.3 424.6 %reduce-scatter.3.cloned.1.call-start = ((), (), s32[]{:S(2)}) async-start(), calls=%async_computation.8 | async-start | bytes 1114112 | tf_op jit(solution)/shard_map/reduce_scatter | solution.py:108
  51.0 116.5 %copy-start.1 = (bf16[128,4096]{1,0:T(8,128)(2,1)S(1)}, bf16[128,4096]{1,0:T(8,128)(2,1)}, u32[]{:S(2)}) copy-start(bf16[128,4096]{1,0:T(8,128)(2,1)} %all-gather.6.cloned.1.call-done) | copy-start | bytes 3145732
  111.9 58.5 %copy-start.5 = (f32[512]{0:T(512)S(1)}, f32[512]{0:T(512)}, u32[]{:S(2)}) copy-start(f32[512]{0:T(512)} %param.23) | copy-start | bytes 6148
  111.9 58.7 %copy-start.2 = (bf16[512,32]{0,1:T(8,128)(2,1)S(1)}, bf16[512,32]{0,1:T(8,128)(2,1)}, u32[]{:S(2)}) copy-start(bf16[512,32]{0,1:T(8,128)(2,1)} %param.24) | copy-start | bytes 98308
  112.0 58.4 %collective-permute-start.1 = (bf16[3,512]{1,0:T(4,128)(2,1)S(1)}, bf16[3,512]{1,0:T(4,128)(2,1)S(1)}, u32[]{:S(2)}, u32[]{:S(2)}) collective-permute-start(bf16[3,512]{1,0:T(4,128)(2,1)S(1)} %slice.48), channel_id=1, source_target_pairs={{0,16},{16,32},{32,48},{48,64},{64,80},{80,96},{96,112},{112,128},... | collective-permute-start | bytes 9224 | tf_op jit(solution)/shard_map/ppermute | solution.py:16
  218.1 129.7 %copy-start.7 = (f32[512]{0:T(512)S(1)}, f32[512]{0:T(512)}, u32[]{:S(2)}) copy-start(f32[512]{0:T(512)} %param.26) | copy-start | bytes 6148
  257.2 3.7 collective-permute-start
  260.9 4.7 collective-permute-start
  265.5 4.7 collective-permute-start
  270.2 5.1 collective-permute-start
  275.3 4.7 collective-permute-start
  280.0 6.9 %collective-permute-start = (f32[512,16]{0,1:T(8,128)S(1)}, f32[512,16]{0,1:T(8,128)S(1)}, u32[]{:S(2)}, u32[]{:S(2)}) collective-permute-start(f32[512,16]{0,1:T(8,128)S(1)} %multiply_add_fusion.3), channel_id=1, source_target_pairs={{0,16},{16,32},{32,48},{48,64},{64,80},{80,96},{96,112},{112,128},... | collective-permute-start | bytes 98312 | tf_op jit(solution)/shard_map/while/body/eval_jaxpr/ppermute | solution.py:16
  286.8 6.7 %collective-permute-start = (f32[512,16]{0,1:T(8,128)S(1)}, f32[512,16]{0,1:T(8,128)S(1)}, u32[]{:S(2)}, u32[]{:S(2)}) collective-permute-start(f32[512,16]{0,1:T(8,128)S(1)} %multiply_add_fusion.3), channel_id=1, source_target_pairs={{0,16},{16,32},{32,48},{48,64},{64,80},{80,96},{96,112},{112,128},... | collective-permute-start | bytes 98312 | tf_op jit(solution)/shard_map/while/body/eval_jaxpr/ppermute | solution.py:16
  293.5 6.8 %collective-permute-start = (f32[512,16]{0,1:T(8,128)S(1)}, f32[512,16]{0,1:T(8,128)S(1)}, u32[]{:S(2)}, u32[]{:S(2)}) collective-permute-start(f32[512,16]{0,1:T(8,128)S(1)} %multiply_add_fusion.3), channel_id=1, source_target_pairs={{0,16},{16,32},{32,48},{48,64},{64,80},{80,96},{96,112},{112,128},... | collective-permute-start | bytes 98312 | tf_op jit(solution)/shard_map/while/body/eval_jaxpr/ppermute | solution.py:16
  300.3 6.8 %collective-permute-start = (f32[512,16]{0,1:T(8,128)S(1)}, f32[512,16]{0,1:T(8,128)S(1)}, u32[]{:S(2)}, u32[]{:S(2)}) collective-permute-start(f32[512,16]{0,1:T(8,128)S(1)} %multiply_add_fusion.3), channel_id=1, source_target_pairs={{0,16},{16,32},{32,48},{48,64},{64,80},{80,96},{96,112},{112,128},... | collective-permute-start | bytes 98312 | tf_op jit(solution)/shard_map/while/body/eval_jaxpr/ppermute | solution.py:16
  307.1 6.8 %collective-permute-start = (f32[512,16]{0,1:T(8,128)S(1)}, f32[512,16]{0,1:T(8,128)S(1)}, u32[]{:S(2)}, u32[]{:S(2)}) collective-permute-start(f32[512,16]{0,1:T(8,128)S(1)} %multiply_add_fusion.3), channel_id=1, source_target_pairs={{0,16},{16,32},{32,48},{48,64},{64,80},{80,96},{96,112},{112,128},... | collective-permute-start | bytes 98312 | tf_op jit(solution)/shard_map/while/body/eval_jaxpr/ppermute | solution.py:16
  313.8 6.8 %collective-permute-start = (f32[512,16]{0,1:T(8,128)S(1)}, f32[512,16]{0,1:T(8,128)S(1)}, u32[]{:S(2)}, u32[]{:S(2)}) collective-permute-start(f32[512,16]{0,1:T(8,128)S(1)} %multiply_add_fusion.3), channel_id=1, source_target_pairs={{0,16},{16,32},{32,48},{48,64},{64,80},{80,96},{96,112},{112,128},... | collective-permute-start | bytes 98312 | tf_op jit(solution)/shard_map/while/body/eval_jaxpr/ppermute | solution.py:16
  320.6 6.9 %collective-permute-start = (f32[512,16]{0,1:T(8,128)S(1)}, f32[512,16]{0,1:T(8,128)S(1)}, u32[]{:S(2)}, u32[]{:S(2)}) collective-permute-start(f32[512,16]{0,1:T(8,128)S(1)} %multiply_add_fusion.3), channel_id=1, source_target_pairs={{0,16},{16,32},{32,48},{48,64},{64,80},{80,96},{96,112},{112,128},... | collective-permute-start | bytes 98312 | tf_op jit(solution)/shard_map/while/body/eval_jaxpr/ppermute | solution.py:16
  327.6 6.6 %collective-permute-start = (f32[512,16]{0,1:T(8,128)S(1)}, f32[512,16]{0,1:T(8,128)S(1)}, u32[]{:S(2)}, u32[]{:S(2)}) collective-permute-start(f32[512,16]{0,1:T(8,128)S(1)} %multiply_add_fusion.3), channel_id=1, source_target_pairs={{0,16},{16,32},{32,48},{48,64},{64,80},{80,96},{96,112},{112,128},... | collective-permute-start | bytes 98312 | tf_op jit(solution)/shard_map/while/body/eval_jaxpr/ppermute | solution.py:16
  334.2 6.8 %collective-permute-start = (f32[512,16]{0,1:T(8,128)S(1)}, f32[512,16]{0,1:T(8,128)S(1)}, u32[]{:S(2)}, u32[]{:S(2)}) collective-permute-start(f32[512,16]{0,1:T(8,128)S(1)} %multiply_add_fusion.3), channel_id=1, source_target_pairs={{0,16},{16,32},{32,48},{48,64},{64,80},{80,96},{96,112},{112,128},... | collective-permute-start | bytes 98312 | tf_op jit(solution)/shard_map/while/body/eval_jaxpr/ppermute | solution.py:16
  340.9 6.8 %collective-permute-start = (f32[512,16]{0,1:T(8,128)S(1)}, f32[512,16]{0,1:T(8,128)S(1)}, u32[]{:S(2)}, u32[]{:S(2)}) collective-permute-start(f32[512,16]{0,1:T(8,128)S(1)} %multiply_add_fusion.3), channel_id=1, source_target_pairs={{0,16},{16,32},{32,48},{48,64},{64,80},{80,96},{96,112},{112,128},... | collective-permute-start | bytes 98312 | tf_op jit(solution)/shard_map/while/body/eval_jaxpr/ppermute | solution.py:16
  347.7 4.5 copy-start.4
  347.7 87.2 %copy-start.3 = (f32[4096]{0:T(1024)S(1)}, f32[4096]{0:T(1024)}, u32[]{:S(2)}) copy-start(f32[4096]{0:T(1024)} %param.28) | copy-start | bytes 49156
  352.1 156.4 %all-gather.14.cloned.1.call-start = ((), (), s32[]{:S(2)}) async-start(), calls=%async_computation.9 | async-start | bytes 4456448 | tf_op jit(solution)/shard_map/all_gather | solution.py:147
  455.3 150.3 %reduce-scatter.5.cloned.1.call-start = ((), (), s32[]{:S(2)}) async-start(), calls=%async_computation.10 | async-start | bytes 4456448 | tf_op jit(solution)/shard_map/reduce_scatter | solution.py:156
  524.8 92.1 %copy-start.6 = (bf16[4096,16]{0,1:T(8,128)(2,1)S(1)}, bf16[4096,16]{0,1:T(8,128)(2,1)}, u32[]{:S(2)}) copy-start(bf16[4096,16]{0,1:T(8,128)(2,1)} %param.29) | copy-start | bytes 393220
  607.5 21.1 %all-to-all-start.1 = ((bf16[16,2,4096]{2,1,0:T(2,128)(2,1)}), bf16[16,2,4096]{2,1,0:T(2,128)(2,1)S(1)}, u32[]{:S(2)}, u32[]{:S(2)}) async-start(bf16[16,2,4096]{2,1,0:T(2,128)(2,1)} %reshape.76), calls=%async_computation.3 | async-start | bytes 524288 | tf_op jit(solution)/shard_map/all_to_all | solution.py:159
Sparse Core Ops, SparseCore 0:
  9.1 41.8 all-gather.5
  53.4 55.2 all-gather.7
  111.1 56.2 all-gather.9
  169.7 61.4 all-gather.11
  352.3 81.6 reduce-scatter.2
  455.4 53.0 all-gather.13
  524.9 80.7 reduce-scatter.4
where the time goes:
time: 637 us; the launch traced here: 636 us
  waiting for transfers between devices  394 us (62%)
  starting transfers between devices  87.9 us (14%)
  matrix products  68.1 us (11%)
  blocking collectives  65.7 us (10%)
  between operations  13.7 us (2%)
    reduce_scatter x1, waiting for transfers between devices, local(): lax.psum_scatter(jnp.dot(blender_result, out_whole, preferred_element_typ...  81.1 us
    reduce_scatter x1, waiting for transfers between devices, local(): lax.psum_scatter(partial_out.astype(jnp.bfloat16), 'ctx', scatter_dimensi...  80.9 us
    ppermute x16, starting transfers between devices, shifted(): return lax.ppermute(shard, axis, pairs)  78.2 us
    all_gather x1, waiting for transfers between devices, local(): lax.all_gather(input_weight, 'ctx', axis=0, tiled=True)  57.7 us
    all_gather x1, waiting for transfers between devices, local(): shard_rows = lax.all_gather(arrived, 'ctx', axis=0, tiled=True)  53 us
    all_gather x1, waiting for transfers between devices, local(): lax.all_gather(gate_weight, 'ctx', axis=0, tiled=True)  52.4 us
    psum x1, blocking collectives, local(): lax.psum(jnp.dot(mixer_in, state_weight, preferred_element_type=jnp.float...  46.7 us
    all_gather x1, waiting for transfers between devices, local(): whole_stretch = lax.all_gather(tokens, 'exp', axis=1, tiled=True)  40.3 us
  transfers between devices with their start and end apart: 24, of which 22 were waited for; matrix products, arithmetic and copies ran while one was open for 8% of the time, Pallas kernels for 0%

commit v1 on v0

--- a/solution.py
+++ b/solution.py
@@ -1,3 +1,4 @@
+import functools
 import jax
 import jax.numpy as jnp
 from jax import lax
@@ -8,6 +9,15 @@
 TOP = 2
 CAP = 2
 precise = lax.Precision.HIGHEST
+
+
+def lane_reach(local_x, axis_name):
+    return jnp.concatenate(
+        lax.all_to_all(jnp.stack(lax.axis_size(axis_name) * [local_x], 0), axis_name, 0, 0), axis=1
+    )
+
+
+track_tracks_over_axis = functools.partial(lane_reach, axis_name="exp")
 
 
 def shifted(shard, axis, by):
@@ -47,7 +57,7 @@
     expert_down,
     expert_ids,
 ):
-    whole_stretch = lax.all_gather(tokens, "exp", axis=1, tiled=True)
+    whole_stretch = track_tracks_over_axis(tokens)
     stretch_rows = whole_stretch.shape[0]
     inner_width = input_weight.shape[1]
     inner_x = jnp.dot(

time: 637 us -> 599 us (0.940)
  waiting for transfers between devices: 394 us -> 345 us
  starting transfers between devices: 87.9 us -> 97.5 us
    all_gather x1 -> x0, waiting for transfers between devices: 40.3 us -> none  [local(): whole_stretch = lax.all_gather(tokens, 'exp', axis=1, tiled=True)]
    all_gather x1, waiting for transfers between devices: 57.7 us -> 22.2 us  [local(): lax.all_gather(input_weight, 'ctx', axis=0, tiled=True)]
    all_to_all x0 -> x1, waiting for transfers between devices: none -> 26.7 us  [lane_reach(): lax.all_to_all(jnp.stack(lax.axis_size(axis_name) * [local_x], 0), axis_n...]
    all_to_all x0 -> x1, starting transfers between devices: none -> 9.98 us  [lane_reach(): lax.all_to_all(jnp.stack(lax.axis_size(axis_name) * [local_x], 0), axis_n...]
where the time goes in v1:
time: 599 us; the launch traced here: 598 us
  waiting for transfers between devices  345 us (58%)
  starting transfers between devices  97.5 us (16%)
  matrix products  67.7 us (11%)
  blocking collectives  66 us (11%)
  between operations  13.7 us (2%)
    reduce_scatter x1, waiting for transfers between devices, local(): lax.psum_scatter(jnp.dot(blender_result, out_whole, preferred_element_typ...  81.5 us
    reduce_scatter x1, waiting for transfers between devices, local(): lax.psum_scatter(partial_out.astype(jnp.bfloat16), 'ctx', scatter_dimensi...  80.9 us
    ppermute x16, starting transfers between devices, shifted(): return lax.ppermute(shard, axis, pairs)  77.8 us
    all_gather x1, waiting for transfers between devices, local(): shard_rows = lax.all_gather(arrived, 'ctx', axis=0, tiled=True)  52.9 us
    all_gather x1, waiting for transfers between devices, local(): lax.all_gather(gate_weight, 'ctx', axis=0, tiled=True)  52.7 us
    psum x1, blocking collectives, local(): lax.psum(jnp.dot(mixer_in, state_weight, preferred_element_type=jnp.float...  46.7 us
    dot_general x4, matrix products, causal_part(): jnp.einsum('ts,tsc,sc->tc', scores, weight, input_block, precision=precise)  38.7 us
    all_to_all x1, waiting for transfers between devices, lane_reach(): lax.all_to_all(jnp.stack(lax.axis_size(axis_name) * [local_x], 0), axis_n...  26.7 us
  transfers between devices with their start and end apart: 24, of which 22 were waited for; matrix products, arithmetic and copies ran while one was open for 8% of the time, Pallas kernels for 0%

profile of v1, /device:TPU:1, one launch (start us, length us, event | category | flops | bytes accessed | tf_op | source)
XLA Modules:
  0.0 598.0 jit_solution(11785369126457917802)
XLA Ops:
  6.5 0.7 all-gather.5.cloned.1.call-update
  7.3 0.7 all-gather.7.cloned.1.call-update
  8.0 2.0 stack.2
  10.0 10.0 %all-to-all-start = ((bf16[16,128,256]{2,1,0:T(8,128)(2,1)}), bf16[16,128,256]{2,1,0:T(8,128)(2,1)S(1)}, u32[]{:S(2)}, u32[]{:S(2)}) async-start(bf16[16,128,256]{2,1,0:T(8,128)(2,1)} %stack.2), calls=%async_computation | async-start | bytes 2097152 | tf_op jit(solution)/shard_map/all_to_all | solution.py:16
  20.0 0.7 all-gather.9.cloned.1.call-update
  20.8 0.4 fusion.45
  21.2 26.7 %all-to-all-done = bf16[16,128,256]{2,1,0:T(8,128)(2,1)S(1)} async-done(((bf16[16,128,256]{2,1,0:T(8,128)(2,1)}), bf16[16,128,256]{2,1,0:T(8,128)(2,1)S(1)}, u32[]{:S(2)}, u32[]{:S(2)}) %all-to-all-start) | async-done | bytes 1048608 | tf_op jit(solution)/shard_map/all_to_all | solution.py:16
  48.0 22.2 %all-gather.5.cloned.1.call-done = bf16[4096,512]{1,0:T(8,128)(2,1)} async-done(((bf16[256,512]{1,0:T(8,128)(2,1)}), bf16[4096,512]{1,0:T(8,128)(2,1)}) %all-gather.5.cloned.1.call-update) | async-done | bytes 4194320 | tf_op jit(solution)/shard_map/all_gather | solution.py:65
  70.2 2.9 convolution_convert_fusion.4
  73.1 3.1 collective-permute-start.1
  76.2 52.7 %all-gather.7.cloned.1.call-done = bf16[4096,512]{1,0:T(8,128)(2,1)} async-done(((bf16[256,512]{1,0:T(8,128)(2,1)}), bf16[4096,512]{1,0:T(8,128)(2,1)}) %all-gather.7.cloned.1.call-update) | async-done | bytes 4194320 | tf_op jit(solution)/shard_map/all_gather | solution.py:70
  128.9 2.9 fusion.30
  132.2 46.7 %psum.7 = f32[128,32]{0,1:T(8,128)S(1)} all-reduce(f32[128,32]{0,1:T(8,128)S(1)} %fusion.70), channel_id=1, replica_groups=mesh['ctx'=16,'exp'=16] {'exp'}, use_global_device_ids=true, to_apply=%region_0.1 | all-reduce | flops 4096 | bytes 32768 | tf_op jit(solution)/shard_map/psum | solution.py:84
  179.2 0.3 fusion.33
  179.5 39.1 %while.20 = (s32[]{:T(128)}, f32[4,128,128]{2,1,0:T(8,128)S(1)}, f32[4,128,128]{2,1,0:T(8,128)S(1)}, f32[4,128,128]{2,1,0:T(8,128)S(1)}, f32[128,128]{1,0:T(8,128)S(1)}, /*index=5*/s32[]{:T(128)}) while((s32[]{:T(128)}, f32[4,128,128]{2,1,0:T(8,128)S(1)}, f32[4,128,128]{2,1,0:T(8,128)S(1)}, f32[4,128,128]{2,1,0:T(8,128)S(1)}, ...), condition=%wide.region_2.3_spmd, body=%wide.region_1.2_spmd.sunk | while | flops 35667968 | bytes 688205 | solution.py:95
  179.6 9.7 %fusion.104 = f32[128,1,128]{2,1,0:T(1,128)S(1)} fusion(f32[128,128,1]{1,2,0:T(1,128)S(1)} %bitcast.96, f32[128,128]{1,0:T(8,128)S(1)} %get-tuple-element.140, f32[128,128]{1,0:T(8,128)S(1)} %get-tuple-element.141, pred[128,128]{1,0:T(8,128)(4,1)S(1)} %iota_compare_fusion.10), kind=kOutput, calls=%fused_computation.clone.1 | convolution fusion | flops 35651584 | bytes 278528 | tf_op jit(solution)/shard_map/while/body/eval_jaxpr/ts,tsc,sc->tc/dot_general | solution.py:40
  189.4 9.7 %fusion.104 = f32[128,1,128]{2,1,0:T(1,128)S(1)} fusion(f32[128,128,1]{1,2,0:T(1,128)S(1)} %bitcast.96, f32[128,128]{1,0:T(8,128)S(1)} %get-tuple-element.140, f32[128,128]{1,0:T(8,128)S(1)} %get-tuple-element.141, pred[128,128]{1,0:T(8,128)(4,1)S(1)} %iota_compare_fusion.10), kind=kOutput, calls=%fused_computation.clone.1 | convolution fusion | flops 35651584 | bytes 278528 | tf_op jit(solution)/shard_map/while/body/eval_jaxpr/ts,tsc,sc->tc/dot_general | solution.py:40
  199.1 9.7 %fusion.104 = f32[128,1,128]{2,1,0:T(1,128)S(1)} fusion(f32[128,128,1]{1,2,0:T(1,128)S(1)} %bitcast.96, f32[128,128]{1,0:T(8,128)S(1)} %get-tuple-element.140, f32[128,128]{1,0:T(8,128)S(1)} %get-tuple-element.141, pred[128,128]{1,0:T(8,128)(4,1)S(1)} %iota_compare_fusion.10), kind=kOutput, calls=%fused_computation.clone.1 | convolution fusion | flops 35651584 | bytes 278528 | tf_op jit(solution)/shard_map/while/body/eval_jaxpr/ts,tsc,sc->tc/dot_general | solution.py:40
  208.9 9.7 %fusion.104 = f32[128,1,128]{2,1,0:T(1,128)S(1)} fusion(f32[128,128,1]{1,2,0:T(1,128)S(1)} %bitcast.96, f32[128,128]{1,0:T(8,128)S(1)} %get-tuple-element.140, f32[128,128]{1,0:T(8,128)S(1)} %get-tuple-element.141, pred[128,128]{1,0:T(8,128)(4,1)S(1)} %iota_compare_fusion.10), kind=kOutput, calls=%fused_computation.clone.1 | convolution fusion | flops 35651584 | bytes 278528 | tf_op jit(solution)/shard_map/while/body/eval_jaxpr/ts,tsc,sc->tc/dot_general | solution.py:40
  218.6 90.2 %while.21 = (s32[]{:T(128)}, f32[512,16]{0,1:T(8,128)S(1)}, f32[512]{0:T(512)S(1)}, f32[512,16]{0,1:T(8,128)S(1)}, s32[]{:T(128)}) while((s32[]{:T(128)}, f32[512,16]{0,1:T(8,128)S(1)}, f32[512]{0:T(512)S(1)}, f32[512,16]{0,1:T(8,128)S(1)}, s32[]{:T(128)}) %tuple.40), condition=%wide.region_4.5_spmd, body=%wide.region_3.4_spmd.sunk | while | flops 16386 | bytes 231525 | solution.py:108
  218.6 2.7 collective-permute-start
  221.3 1.0 collective-permute-done
  222.4 3.6 collective-permute-start
  226.0 1.0 collective-permute-done
  227.0 3.6 collective-permute-start
  230.7 1.0 collective-permute-done
  231.7 3.6 collective-permute-start
  235.3 1.0 collective-permute-done
  236.3 3.7 collective-permute-start
  240.1 1.0 collective-permute-done
  241.1 5.9 collective-permute-start
  247.0 1.0 collective-permute-done
  248.0 5.6 collective-permute-start
  253.6 1.0 collective-permute-done
  254.6 5.8 collective-permute-start
  260.4 1.0 collective-permute-done
  261.4 5.8 collective-permute-start
  267.2 1.0 collective-permute-done
  268.2 5.8 collective-permute-start
  273.9 1.0 collective-permute-done
  274.9 5.8 collective-permute-start
  280.7 1.0 collective-permute-done
  281.7 5.8 collective-permute-start
  287.5 1.2 collective-permute-done
  288.6 5.6 collective-permute-start
  294.2 1.0 collective-permute-done
  295.3 5.8 collective-permute-start
  301.0 1.0 collective-permute-done
  302.0 5.8 collective-permute-start
  307.8 1.0 collective-permute-done
  308.8 0.5 fusion.29
  309.3 3.9 convolution_convert_fusion.1
  313.9 81.5 %reduce-scatter.3.cloned.1.call-done = bf16[8,4096]{1,0:T(8,128)(2,1)} async-done(((bf16[128,4096]{1,0:T(8,128)(2,1)}), bf16[8,4096]{1,0:T(8,128)(2,1)}) %reduce-scatter.3.cloned.1.call-update) | async-done | bytes 65552 | tf_op jit(solution)/shard_map/reduce_scatter | solution.py:118
  395.4 1.0 fusion.41
  396.9 19.3 %all_to_all.15 = bf16[16,2,4096]{2,1,0:T(2,128)(2,1)S(1)} all-to-all(bf16[16,2,4096]{2,1,0:T(2,128)(2,1)S(1)} %reshape.84), channel_id=1, replica_groups=mesh['ctx'=16,'exp'=16] {'exp'}, dimensions={0} | all-to-all | bytes 524288 | tf_op jit(solution)/shard_map/all_to_all | solution.py:152
  416.2 0.8 reshape.85
  417.2 52.9 %all-gather.11.cloned.1.call-done = bf16[512,4096]{1,0:T(8,128)(2,1)} async-done(((bf16[32,4096]{1,0:T(8,128)(2,1)}), bf16[512,4096]{1,0:T(8,128)(2,1)}) %all-gather.11.cloned.1.call-update) | async-done | bytes 4194320 | tf_op jit(solution)/shard_map/all_gather | solution.py:157
  470.2 5.4 fusion.18
  475.6 10.8 %convolution_convert_fusion = bf16[512,4096]{1,0:T(8,128)(2,1)} fusion(bf16[1,448,4096]{2,1,0:T(8,128)(2,1)} %param.32, bf16[512,4096]{1,0:T(8,128)(2,1)} %all-gather.11.cloned.1.call-done, bf16[1,448,4096]{2,1,0:T(8,128)(2,1)} %param.31, f32[512,448]{0,1:T(8,128)S(1)} %fusion.18), kind=kOutput, calls=%fused_computation.19 | convolution fusion | flops 3761569792 | bytes 16646144 | tf_op jit(solution)/shard_map/dot_general | solution.py:165
  486.4 80.9 %reduce-scatter.5.cloned.1.call-done = bf16[32,4096]{1,0:T(8,128)(2,1)} async-done(((bf16[512,4096]{1,0:T(8,128)(2,1)}), bf16[32,4096]{1,0:T(8,128)(2,1)}) %reduce-scatter.5.cloned.1.call-update) | async-done | bytes 262160 | tf_op jit(solution)/shard_map/reduce_scatter | solution.py:166
  567.2 1.8 reshape.86
  569.1 9.4 %all-to-all-start.2 = ((bf16[16,2,4096]{2,1,0:T(2,128)(2,1)}), bf16[16,2,4096]{2,1,0:T(2,128)(2,1)S(1)}, u32[]{:S(2)}, u32[]{:S(2)}) async-start(bf16[16,2,4096]{2,1,0:T(2,128)(2,1)} %reshape.86), calls=%async_computation.4 | async-start | bytes 524288 | tf_op jit(solution)/shard_map/all_to_all | solution.py:169
  578.9 11.2 %all-to-all-done.2 = bf16[16,2,4096]{2,1,0:T(2,128)(2,1)S(1)} async-done(((bf16[16,2,4096]{2,1,0:T(2,128)(2,1)}), bf16[16,2,4096]{2,1,0:T(2,128)(2,1)S(1)}, u32[]{:S(2)}, u32[]{:S(2)}) %all-to-all-start.2) | async-done | bytes 262176 | tf_op jit(solution)/shard_map/all_to_all | solution.py:169
  590.3 0.9 fusion.14
  (83 shorter events, 3.2 us)
Async XLA Ops:
  6.5 14.2 %copy-start = (f32[128,512]{1,0:T(8,128)S(1)}, f32[128,512]{1,0:T(8,128)}, u32[]{:S(2)}) copy-start(f32[128,512]{1,0:T(8,128)} %param.25) | copy-start | bytes 786436
  6.5 14.6 %copy-start.3 = (f32[4,512]{1,0:T(4,128)S(1)}, f32[4,512]{1,0:T(4,128)}, u32[]{:S(2)}) copy-start(f32[4,512]{1,0:T(4,128)} %param.22) | copy-start | bytes 24580
  6.5 63.6 %all-gather.5.cloned.1.call-start = ((), (), s32[]{:S(2)}) async-start(), calls=%async_computation.5 | async-start | bytes 4456448 | tf_op jit(solution)/shard_map/all_gather | solution.py:65
  7.3 121.7 %all-gather.7.cloned.1.call-start = ((), (), s32[]{:S(2)}) async-start(), calls=%async_computation.6 | async-start | bytes 4456448 | tf_op jit(solution)/shard_map/all_gather | solution.py:70
  10.0 37.9 %all-to-all-start = ((bf16[16,128,256]{2,1,0:T(8,128)(2,1)}), bf16[16,128,256]{2,1,0:T(8,128)(2,1)S(1)}, u32[]{:S(2)}, u32[]{:S(2)}) async-start(bf16[16,128,256]{2,1,0:T(8,128)(2,1)} %stack.2), calls=%async_computation | async-start | bytes 2097152 | tf_op jit(solution)/shard_map/all_to_all | solution.py:16
  20.0 289.3 %all-gather.9.cloned.1.call-start = ((), (), s32[]{:S(2)}) async-start(), calls=%async_computation.7 | async-start | bytes 4456448 | tf_op jit(solution)/shard_map/all_gather | solution.py:117
  20.7 374.7 %reduce-scatter.3.cloned.1.call-start = ((), (), s32[]{:S(2)}) async-start(), calls=%async_computation.8 | async-start | bytes 1114112 | tf_op jit(solution)/shard_map/reduce_scatter | solution.py:118
  73.1 58.8 %copy-start.5 = (f32[512]{0:T(512)S(1)}, f32[512]{0:T(512)}, u32[]{:S(2)}) copy-start(f32[512]{0:T(512)} %param.23) | copy-start | bytes 6148
  73.1 59.0 %copy-start.1 = (bf16[512,32]{0,1:T(8,128)(2,1)S(1)}, bf16[512,32]{0,1:T(8,128)(2,1)}, u32[]{:S(2)}) copy-start(bf16[512,32]{0,1:T(8,128)(2,1)} %param.24) | copy-start | bytes 98308
  73.1 58.7 %collective-permute-start.1 = (bf16[3,512]{1,0:T(4,128)(2,1)S(1)}, bf16[3,512]{1,0:T(4,128)(2,1)S(1)}, u32[]{:S(2)}, u32[]{:S(2)}) collective-permute-start(bf16[3,512]{1,0:T(4,128)(2,1)S(1)} %slice.48), channel_id=1, source_target_pairs={{0,16},{16,32},{32,48},{48,64},{64,80},{80,96},{96,112},{112,128},... | collective-permute-start | bytes 9224 | tf_op jit(solution)/shard_map/ppermute | solution.py:26
  179.5 129.3 %copy-start.7 = (f32[512]{0:T(512)S(1)}, f32[512]{0:T(512)}, u32[]{:S(2)}) copy-start(f32[512]{0:T(512)} %param.26) | copy-start | bytes 6148
  218.6 3.7 collective-permute-start
  222.4 4.7 collective-permute-start
  227.0 4.7 collective-permute-start
  231.7 4.7 collective-permute-start
  236.3 4.7 collective-permute-start
  241.1 6.9 %collective-permute-start = (f32[512,16]{0,1:T(8,128)S(1)}, f32[512,16]{0,1:T(8,128)S(1)}, u32[]{:S(2)}, u32[]{:S(2)}) collective-permute-start(f32[512,16]{0,1:T(8,128)S(1)} %multiply_add_fusion.3), channel_id=1, source_target_pairs={{0,16},{16,32},{32,48},{48,64},{64,80},{80,96},{96,112},{112,128},... | collective-permute-start | bytes 98312 | tf_op jit(solution)/shard_map/while/body/eval_jaxpr/ppermute | solution.py:26
  248.0 6.6 %collective-permute-start = (f32[512,16]{0,1:T(8,128)S(1)}, f32[512,16]{0,1:T(8,128)S(1)}, u32[]{:S(2)}, u32[]{:S(2)}) collective-permute-start(f32[512,16]{0,1:T(8,128)S(1)} %multiply_add_fusion.3), channel_id=1, source_target_pairs={{0,16},{16,32},{32,48},{48,64},{64,80},{80,96},{96,112},{112,128},... | collective-permute-start | bytes 98312 | tf_op jit(solution)/shard_map/while/body/eval_jaxpr/ppermute | solution.py:26
  254.6 6.8 %collective-permute-start = (f32[512,16]{0,1:T(8,128)S(1)}, f32[512,16]{0,1:T(8,128)S(1)}, u32[]{:S(2)}, u32[]{:S(2)}) collective-permute-start(f32[512,16]{0,1:T(8,128)S(1)} %multiply_add_fusion.3), channel_id=1, source_target_pairs={{0,16},{16,32},{32,48},{48,64},{64,80},{80,96},{96,112},{112,128},... | collective-permute-start | bytes 98312 | tf_op jit(solution)/shard_map/while/body/eval_jaxpr/ppermute | solution.py:26
  261.4 6.8 %collective-permute-start = (f32[512,16]{0,1:T(8,128)S(1)}, f32[512,16]{0,1:T(8,128)S(1)}, u32[]{:S(2)}, u32[]{:S(2)}) collective-permute-start(f32[512,16]{0,1:T(8,128)S(1)} %multiply_add_fusion.3), channel_id=1, source_target_pairs={{0,16},{16,32},{32,48},{48,64},{64,80},{80,96},{96,112},{112,128},... | collective-permute-start | bytes 98312 | tf_op jit(solution)/shard_map/while/body/eval_jaxpr/ppermute | solution.py:26
  268.2 6.8 %collective-permute-start = (f32[512,16]{0,1:T(8,128)S(1)}, f32[512,16]{0,1:T(8,128)S(1)}, u32[]{:S(2)}, u32[]{:S(2)}) collective-permute-start(f32[512,16]{0,1:T(8,128)S(1)} %multiply_add_fusion.3), channel_id=1, source_target_pairs={{0,16},{16,32},{32,48},{48,64},{64,80},{80,96},{96,112},{112,128},... | collective-permute-start | bytes 98312 | tf_op jit(solution)/shard_map/while/body/eval_jaxpr/ppermute | solution.py:26
  274.9 6.8 %collective-permute-start = (f32[512,16]{0,1:T(8,128)S(1)}, f32[512,16]{0,1:T(8,128)S(1)}, u32[]{:S(2)}, u32[]{:S(2)}) collective-permute-start(f32[512,16]{0,1:T(8,128)S(1)} %multiply_add_fusion.3), channel_id=1, source_target_pairs={{0,16},{16,32},{32,48},{48,64},{64,80},{80,96},{96,112},{112,128},... | collective-permute-start | bytes 98312 | tf_op jit(solution)/shard_map/while/body/eval_jaxpr/ppermute | solution.py:26
  281.7 6.9 %collective-permute-start = (f32[512,16]{0,1:T(8,128)S(1)}, f32[512,16]{0,1:T(8,128)S(1)}, u32[]{:S(2)}, u32[]{:S(2)}) collective-permute-start(f32[512,16]{0,1:T(8,128)S(1)} %multiply_add_fusion.3), channel_id=1, source_target_pairs={{0,16},{16,32},{32,48},{48,64},{64,80},{80,96},{96,112},{112,128},... | collective-permute-start | bytes 98312 | tf_op jit(solution)/shard_map/while/body/eval_jaxpr/ppermute | solution.py:26
  288.6 6.6 %collective-permute-start = (f32[512,16]{0,1:T(8,128)S(1)}, f32[512,16]{0,1:T(8,128)S(1)}, u32[]{:S(2)}, u32[]{:S(2)}) collective-permute-start(f32[512,16]{0,1:T(8,128)S(1)} %multiply_add_fusion.3), channel_id=1, source_target_pairs={{0,16},{16,32},{32,48},{48,64},{64,80},{80,96},{96,112},{112,128},... | collective-permute-start | bytes 98312 | tf_op jit(solution)/shard_map/while/body/eval_jaxpr/ppermute | solution.py:26
  295.3 6.8 %collective-permute-start = (f32[512,16]{0,1:T(8,128)S(1)}, f32[512,16]{0,1:T(8,128)S(1)}, u32[]{:S(2)}, u32[]{:S(2)}) collective-permute-start(f32[512,16]{0,1:T(8,128)S(1)} %multiply_add_fusion.3), channel_id=1, source_target_pairs={{0,16},{16,32},{32,48},{48,64},{64,80},{80,96},{96,112},{112,128},... | collective-permute-start | bytes 98312 | tf_op jit(solution)/shard_map/while/body/eval_jaxpr/ppermute | solution.py:26
  302.0 6.8 %collective-permute-start = (f32[512,16]{0,1:T(8,128)S(1)}, f32[512,16]{0,1:T(8,128)S(1)}, u32[]{:S(2)}, u32[]{:S(2)}) collective-permute-start(f32[512,16]{0,1:T(8,128)S(1)} %multiply_add_fusion.3), channel_id=1, source_target_pairs={{0,16},{16,32},{32,48},{48,64},{64,80},{80,96},{96,112},{112,128},... | collective-permute-start | bytes 98312 | tf_op jit(solution)/shard_map/while/body/eval_jaxpr/ppermute | solution.py:26
  308.8 4.5 copy-start.4
  308.8 87.6 %copy-start.2 = (f32[4096]{0:T(1024)S(1)}, f32[4096]{0:T(1024)}, u32[]{:S(2)}) copy-start(f32[4096]{0:T(1024)} %param.28) | copy-start | bytes 49156
  313.2 156.9 %all-gather.11.cloned.1.call-start = ((), (), s32[]{:S(2)}) async-start(), calls=%async_computation.9 | async-start | bytes 4456448 | tf_op jit(solution)/shard_map/all_gather | solution.py:157
  417.0 150.2 %reduce-scatter.5.cloned.1.call-start = ((), (), s32[]{:S(2)}) async-start(), calls=%async_computation.10 | async-start | bytes 4456448 | tf_op jit(solution)/shard_map/reduce_scatter | solution.py:166
  486.3 92.1 %copy-start.6 = (bf16[4096,16]{0,1:T(8,128)(2,1)S(1)}, bf16[4096,16]{0,1:T(8,128)(2,1)}, u32[]{:S(2)}) copy-start(bf16[4096,16]{0,1:T(8,128)(2,1)} %param.29) | copy-start | bytes 393220
  569.1 21.1 %all-to-all-start.2 = ((bf16[16,2,4096]{2,1,0:T(2,128)(2,1)}), bf16[16,2,4096]{2,1,0:T(2,128)(2,1)S(1)}, u32[]{:S(2)}, u32[]{:S(2)}) async-start(bf16[16,2,4096]{2,1,0:T(2,128)(2,1)} %reshape.86), calls=%async_computation.4 | async-start | bytes 524288 | tf_op jit(solution)/shard_map/all_to_all | solution.py:169
Sparse Core Ops, SparseCore 0:
  9.8 60.3 all-gather.4
  72.6 56.2 all-gather.6
  131.3 61.4 all-gather.8
  313.4 82.0 reduce-scatter.2
  417.1 52.9 all-gather.10
  486.5 80.7 reduce-scatter.4
